TPU v7x, 256 devices: a whole 4x4x8 slice. The times are simulated.
256 devices in a mesh: across: 4 (over x), along: 8 (over z), gas: 8 (over y, core).
Axes of the slice: x: 4, y: 4, z: 8, core: 2. Of those that a mesh axis runs over, the one named last changes fastest.
Arguments:
- gas_vel: float32 [2, 2048, 1024], P(None, ('along', 'gas'), 'across'), may hold values from -0.5 to 1.5
- viscosity: float32 [2048, 1024], P(('along', 'gas'), 'across'), may hold values from 0.05 to 0.5
- positions: float32 [2, 128, 64, 128], P(None, 'along', ('across', 'gas')), may hold values from 0 to 1
- velocities: float32 [2, 128, 64, 128], P(None, 'along', ('across', 'gas')), may hold values from -4 to 4
- radius: float32 [128, 64, 128], P('along', ('across', 'gas')), may hold values from 0.5 to 0.9
- drag_coef: float32 [128, 64, 128], P('along', ('across', 'gas')), may hold values from 0.5 to 4
- counts: int32 [128, 64], P('along', ('across', 'gas')), may hold values from 16 to 128
- pattern: int32 [128, 64, 9], P('along', ('across', 'gas')), may hold values 0 or 1
- cell_index: int32 [128, 64, 128], P('along', ('across', 'gas')), may hold values from 0 to 238, as said below
- cell_frac: int32 [2, 128, 64, 128], P(None, 'along', ('across', 'gas')), may hold values from 0 to 1024
Outputs:
- particles_out: float32 [4, 128, 64, 128], P(None, 'along', ('across', 'gas'))
- gas_out: float32 [2, 2048, 1024], P(None, ('along', 'gas'), 'across')
Inputs may be any that keep to these rules, and one draw needn't show every extreme that they name: `cell_index`: row*16 + col with row and col each from 0 to 14.
All inputs are finite; a program needn't handle non-finite values. Where the computation divides by a largest or mean magnitude, that divisor is 1e-20 or more. No bound on the sum of `pattern` on one device may be relied on, other than what follows from the above.
Results may differ from a plain program's by a relative error of at most 0.0003.
Values sent between devices are 32-bit elements; how exact they have to be, the bound alone decides.
A program may use at most 64 MiB of HBM per device.

v0:
```python
import jax
import jax.numpy as jnp
from jax import lax
from jax.sharding import Mesh
from jax.sharding import PartitionSpec as P

CELL_EDGE = 16
ACROSS_ALONG_GAS = ("across", "along", "gas_0", "gas_1")
GAS = ("gas_0", "gas_1")
ACROSS_GAS = ("across", "gas_0", "gas_1")
ALONG_GAS = ("along", "gas_0", "gas_1")


offsets = [(-1, -1), (-1, 0), (-1, 1), (0, -1), (0, 0), (0, 1), (1, -1), (1, 0), (1, 1)]
stiffness = 40.0
damping = 2.0
gravity = 1.0
courant = 0.4
softening = 0.0001
density = 0.36
frac_unit = 1024.0


def by_axis(x, axes):
    for axis in axes:
        x = lax.pmax(x, axis)
    return x


def extended_2(x, sides, width, wrap):
    for axis, dim in sides:
        size, length = (lax.axis_size(axis), x.shape[dim])
        up = [(i, (i + 1) % size) for i in range(size if wrap else size - 1)]
        down = [(j, i) for i, j in up]
        last = lax.slice_in_dim(x, length - width, length, axis=dim)
        first = lax.slice_in_dim(x, 0, width, axis=dim)
        before = lax.ppermute(last, axis, up)
        after = lax.ppermute(first, axis, down)
        x = jnp.concatenate([before, x, after], axis=dim)
    return x


def padded(x, sides, width, wrap):
    edges = {}
    for axis, dim in sides:
        size, length = (lax.axis_size(axis), x.shape[dim])
        up = [(i, (i + 1) % size) for i in range(size if wrap else size - 1)]
        last = lax.slice_in_dim(x, length - width, length, axis=dim)
        first = lax.slice_in_dim(x, 0, width, axis=dim)
        edges[dim] = (
            lax.ppermute(last, axis, up),
            lax.ppermute(first, axis, [(b, a) for a, b in up]),
        )
    done = []
    for _, dim in sides:
        low, high = edges[dim]
        around = [(width, width) if d in done else (0, 0) for d in range(x.ndim)]
        x = jnp.concatenate([jnp.pad(low, around), x, jnp.pad(high, around)], axis=dim)
        done.append(dim)
    return x


def over_axes(x, axes):
    for axis in axes:
        x = lax.psum(x, axis)
    return x


def contact(extended, tile_mask, cell_edge):
    tile_rows = tile_mask.shape[0]
    tile_cols = tile_mask.shape[1]
    centre = extended[:, 1 : 1 + tile_rows, 1 : 1 + tile_cols]
    mine = centre[..., :, None]
    forces_z = jnp.zeros(centre.shape[1:], jnp.float32)
    forces_x = jnp.zeros(centre.shape[1:], jnp.float32)
    for neighbour, (shift_z, shift_x) in enumerate(offsets):
        partner = extended[
            :, 1 + shift_z : 1 + shift_z + tile_rows, 1 + shift_x : 1 + shift_x + tile_cols
        ][..., None, :]
        apart_z = mine[0] - partner[0] - shift_z * cell_edge
        apart_x = mine[1] - partner[1] - shift_x * cell_edge
        distance = jnp.sqrt(apart_z * apart_z + apart_x * apart_x + softening)
        depth = jnp.maximum(mine[4] + partner[4] - distance, 0.0)
        closing = ((mine[2] - partner[2]) * apart_z + (mine[3] - partner[3]) * apart_x) / distance
        strength = (
            depth
            * (stiffness - damping * closing)
            / distance
            * (mine[5] * partner[5])
            * tile_mask[:, :, neighbour][:, :, None, None]
        )
        forces_z = forces_z + jnp.sum(strength * apart_z, axis=-1)
        forces_x = forces_x + jnp.sum(strength * apart_x, axis=-1)
    return (forces_z, forces_x)


def update(centre, coupling, forces_z, forces_x, sub_step):
    alive_mask = centre[5]
    inverse = alive_mask * density / (centre[4] * centre[4] + 1.0 - alive_mask)
    drag_z = coupling[2] * (coupling[0] - centre[2])
    drag_x = coupling[2] * (coupling[1] - centre[3])
    speed_z = centre[2] + sub_step * (inverse * (forces_z + drag_z) - gravity * alive_mask)
    speed_x = centre[3] + sub_step * (inverse * (forces_x + drag_x))
    moved = jnp.stack(
        [
            centre[0] + sub_step * speed_z,
            centre[1] + sub_step * speed_x,
            speed_z,
            speed_x,
            centre[4],
            alive_mask,
        ]
    )
    return (moved, jnp.stack([alive_mask * drag_z, alive_mask * drag_x]))


def stencil(cell_index, cell_frac, cell_edge):
    share_z = cell_frac[0].astype(jnp.float32) / frac_unit
    share_x = cell_frac[1].astype(jnp.float32) / frac_unit
    cell_ids = jnp.arange(cell_edge * cell_edge, dtype=jnp.int32)
    corner = cell_index[..., None]
    result = ((1.0 - share_z) * (1.0 - share_x))[..., None] * (cell_ids == corner).astype(
        jnp.float32
    )
    result = result + (share_z * (1.0 - share_x))[..., None] * (
        cell_ids == corner + cell_edge
    ).astype(jnp.float32)
    result = result + ((1.0 - share_z) * share_x)[..., None] * (cell_ids == corner + 1).astype(
        jnp.float32
    )
    result = result + (share_z * share_x)[..., None] * (cell_ids == corner + cell_edge + 1).astype(
        jnp.float32
    )
    return result


def gas_update(velocity, viscosity, padded_rows, padded_cols, source, gas_step):
    upper_row = padded_rows[:, 2:]
    lower_row = padded_rows[:, :-2]
    right_col = padded_cols[:, :, 2:]
    left_col = padded_cols[:, :, :-2]
    laplace = upper_row + lower_row + right_col + left_col - 4.0 * velocity
    advect = (
        velocity[0:1] * (upper_row - lower_row) * 0.5 + velocity[1:2] * (right_col - left_col) * 0.5
    )
    return velocity + gas_step * (viscosity[None] * laplace - advect + source)


def body(
    gas_vel,
    viscosity,
    positions,
    velocities,
    radius,
    drag_coef,
    counts,
    pattern,
    cell_index,
    cell_frac,
):
    local_rate = jnp.max(jnp.abs(gas_vel[0]) + jnp.abs(gas_vel[1]) + 4.0 * viscosity)
    global_rate = by_axis(local_rate, ACROSS_ALONG_GAS)
    gas_step = courant / global_rate
    sub_step = 0.5 * gas_step
    tiles_z = counts.shape[0]
    tiles_x = counts.shape[1]
    slots = radius.shape[2]
    cell_edge = CELL_EDGE
    block_velocity = lax.all_to_all(gas_vel, GAS, split_axis=2, concat_axis=1, tiled=True)
    tile_velocity = block_velocity.reshape(2, tiles_z, cell_edge, tiles_x, cell_edge).transpose(
        0, 1, 3, 2, 4
    )
    tile_velocity = tile_velocity.reshape(2, tiles_z, tiles_x, cell_edge * cell_edge)
    weights = stencil(cell_index, cell_frac, cell_edge)
    interp = jnp.einsum("ztpc,kztc->kztp", weights, tile_velocity, precision=lax.Precision.HIGHEST)
    alive_mask = (jnp.arange(slots, dtype=jnp.int32)[None, None, :] < counts[:, :, None]).astype(
        jnp.float32
    )
    particle_state = jnp.stack(
        [
            positions[0] * cell_edge,
            positions[1] * cell_edge,
            velocities[0],
            velocities[1],
            radius,
            alive_mask,
        ]
    )
    coupling = jnp.stack([interp[0], interp[1], drag_coef])
    tile_mask = pattern.astype(jnp.float32)
    drag_sum = jnp.zeros((2, tiles_z, tiles_x, slots), jnp.float32)
    for substep in range(2):
        extended = extended_2(particle_state, (("along", 1),), 1, True)
        extended = padded(extended, ((ACROSS_GAS, 2),), 1, False)
        forces_z, forces_x = contact(extended, tile_mask, cell_edge)
        particle_state, drag = update(particle_state, coupling, forces_z, forces_x, sub_step)
        drag_sum = drag_sum + drag
    mean_drag = 0.5 * drag_sum
    summed = over_axes(jnp.sum(mean_drag, axis=(1, 2, 3)), ACROSS_ALONG_GAS)
    deposit = jnp.einsum("ztpc,kztp->kztc", weights, mean_drag, precision=lax.Precision.HIGHEST)
    block_deposit = deposit.reshape(2, tiles_z, tiles_x, cell_edge, cell_edge).transpose(
        0, 1, 3, 2, 4
    )
    block_deposit = block_deposit.reshape(2, tiles_z * cell_edge, tiles_x * cell_edge)
    gas_deposit = lax.all_to_all(block_deposit, GAS, split_axis=1, concat_axis=2, tiled=True)
    cells_all = (
        gas_deposit.shape[1]
        * gas_deposit.shape[2]
        * lax.axis_size("across")
        * lax.axis_size("along")
        * lax.axis_size(GAS)
    )
    source = summed[:, None, None] / cells_all - gas_deposit
    padded_rows = padded(gas_vel, ((ALONG_GAS, 1),), 1, True)
    padded_cols = extended_2(gas_vel, (("across", 2),), 1, False)
    gas_out = gas_update(gas_vel, viscosity, padded_rows, padded_cols, source, gas_step)
    particles_out = jnp.stack(
        [
            particle_state[0] / cell_edge,
            particle_state[1] / cell_edge,
            particle_state[2],
            particle_state[3],
        ]
    )
    return (particles_out, gas_out)


def solution(mesh):
    split = Mesh(
        mesh.devices.reshape(mesh.shape["across"], mesh.shape["along"], 4, 2),
        ("across", "along", "gas_0", "gas_1"),
    )
    return jax.shard_map(
        body,
        mesh=split,
        in_specs=(
            P(None, ALONG_GAS, "across"),
            P(ALONG_GAS, "across"),
            P(None, "along", ACROSS_GAS, None),
            P(None, "along", ACROSS_GAS, None),
            P("along", ACROSS_GAS, None),
            P("along", ACROSS_GAS, None),
            P("along", ACROSS_GAS),
            P("along", ACROSS_GAS, None),
            P("along", ACROSS_GAS, None),
            P(None, "along", ACROSS_GAS, None),
        ),
        out_specs=(P(None, "along", ACROSS_GAS, None), P(None, ALONG_GAS, "across")),
        check_vma=False,
    )
```

profile of v0, /device:TPU:1, one launch (start us, length us, event | category | flops | bytes accessed | tf_op | source)
XLA Modules:
  0.0 246.2 jit_solution(9847962648812155435)
XLA Ops:
  0.7 1.0 copy.89
  1.8 0.9 reshape.469
  2.7 6.6 %all-to-all-start = ((f32[8,1,2048]{2,1,0:T(1,128)}), f32[8,1,2048]{2,1,0:T(1,128)S(1)}, u32[]{:S(2)}, u32[]{:S(2)}) async-start(f32[8,1,2048]{2,1,0:T(1,128)} %reshape.469), calls=%async_computation | async-start | bytes 131072 | tf_op jit(solution)/shard_map/all_to_all | solution.py:169
  9.5 5.2 %collective-permute-start.1 = (f32[6,1,2,128]{3,2,1,0:T(2,128)S(1)}, f32[6,1,2,128]{3,2,1,0:T(2,128)S(1)}, u32[]{:S(2)}, u32[]{:S(2)}) collective-permute-start(f32[6,1,2,128]{3,2,1,0:T(2,128)S(1)} %get-tuple-element.161), channel_id=1, source_target_pairs={{8,0},{16,8},{24,16},{32,24},{40,32},{48,40},{56,48},{0,56},{9,1},... | collective-permute-start | bytes 18440 | tf_op jit(solution)/shard_map/ppermute | solution.py:38
  14.8 3.1 %collective-permute-start.11 = (f32[2,32,1]{2,1,0:T(8,128)S(1)}, f32[2,32,1]{2,1,0:T(8,128)S(1)}, u32[]{:S(2)}, u32[]{:S(2)}) collective-permute-start(f32[2,32,1]{2,1,0:T(8,128)S(1)} %get-tuple-element.169), channel_id=1, source_target_pairs={{0,64},{64,128},{128,192},{1,65},{65,129},{129,193},{2,66},{66,130... | collective-permute-start | bytes 776 | tf_op jit(solution)/shard_map/ppermute | solution.py:37
  17.9 1.3 collective-permute-start.10
  19.2 0.6 collective-permute-start.8
  19.9 0.6 add_reduce_fusion
  20.6 10.3 %pmax.28 = f32[]{:T(128)} all-reduce(f32[]{:T(128)} %add_reduce_fusion), channel_id=1, replica_groups=mesh['across'=4,'along'=8,'gas_0'=4,'gas_1'=2] {'across'}, use_global_device_ids=true, to_apply=%region_1.0 | all-reduce | flops 1 | bytes 8 | tf_op jit(solution)/shard_map/pmax | solution.py:26
  30.8 14.5 %pmax.29 = f32[]{:T(128)} all-reduce(f32[]{:T(128)} %pmax.28), channel_id=1, replica_groups=mesh['across'=4,'along'=8,'gas_0'=4,'gas_1'=2] {'along'}, use_global_device_ids=true, to_apply=%region_2.0 | all-reduce | flops 1 | bytes 8 | tf_op jit(solution)/shard_map/pmax | solution.py:26
  45.4 9.3 %pmax.30 = f32[]{:T(128)} all-reduce(f32[]{:T(128)} %pmax.29), channel_id=1, replica_groups=mesh['across'=4,'along'=8,'gas_0'=4,'gas_1'=2] {'gas_0'}, use_global_device_ids=true, to_apply=%region_3.0 | all-reduce | flops 1 | bytes 8 | tf_op jit(solution)/shard_map/pmax | solution.py:26
  54.7 10.6 %pmax.31 = f32[]{:T(128)} all-reduce(f32[]{:T(128)} %pmax.30), channel_id=1, replica_groups=mesh['across'=4,'along'=8,'gas_0'=4,'gas_1'=2] {'gas_1'}, use_global_device_ids=true, to_apply=%region_4.0 | all-reduce | flops 1 | bytes 8 | tf_op jit(solution)/shard_map/pmax | solution.py:26
  67.0 1.9 collective-permute-start.2
  68.9 2.6 %collective-permute-start.3 = (f32[6,18,1,128]{3,2,1,0:T(1,128)S(1)}, f32[6,18,1,128]{3,2,1,0:T(1,128)S(1)}, u32[]{:S(2)}, u32[]{:S(2)}) collective-permute-start(f32[6,18,1,128]{3,2,1,0:T(1,128)S(1)} %get-tuple-element.133), channel_id=1, source_target_pairs={{1,0},{2,1},{3,2},{4,3},{5,4},{6,5},{7,6},{64,7},{65,64},{66,65},{... | collective-permute-start | bytes 165896 | tf_op jit(solution)/shard_map/ppermute | solution.py:52
  71.5 8.2 %multiply_reduce_fusion.22 = (f32[16,2,128]{2,1,0:T(2,128)S(1)}, f32[16,2,128]{2,1,0:T(2,128)S(1)}, f32[16,2,128]{2,1,0:T(2,128)S(1)}, f32[16,2,128]{2,1,0:T(2,128)S(1)}) fusion(f32[16,2,128]{2,1,0:T(2,128)S(1)} %get-tuple-element.151, f32[16,2,128]{2,1,0:T(2,128)S(1)} %get-tuple-element.176, f32[16,2]{1,0:T(8,128)S(1)} %copy.81, ...), kind=kLoop, calls=%fused_computation.228 | loop fusion | flops 27770880 | bytes 262400 | tf_op jit(solution)/shard_map/reduce_sum | solution.py:92
  79.8 5.7 %multiply_reduce_fusion.19 = (f32[16,2,128]{2,1,0:T(2,128)S(1)}, f32[16,2,128]{2,1,0:T(2,128)S(1)}) fusion(f32[16,2,128]{2,1,0:T(2,128)S(1)} %get-tuple-element.156, f32[16,2,128]{2,1,0:T(2,128)S(1)} %get-tuple-element.176, f32[16,2]{1,0:T(8,128)S(1)} %copy.87, f32[16,2,128]{2,1,0:T(2,128)S(1)} %get-tuple-element.157, f32[16,2,128]{2,1,0:T(2,128)S(1)} %fusion.134, ...), kind=kLoop, calls=%fused_computation.213 | loop fusion | flops 14147584 | bytes 229504 | tf_op jit(solution)/shard_map/reduce_sum | solution.py:92
  85.5 0.5 broadcast.763
  86.0 0.8 reduce
  88.0 10.2 %fusion.127 = f32[2,16,2,128]{3,0,2,1:T(2,128)S(1)} fusion(f32[2,16,2,256]{3,0,2,1:T(2,128)S(1)} %reshape.466, f32[16,2,128]{2,1,0:T(2,128)S(1)} %get-tuple-element.182, s32[16,2,128]{2,1,0:T(2,128)S(1)} %get-tuple-element.184, f32[16,2,128]{2,1,0:T(2,128)S(1)} %get-tuple-element.181, s32[16,2,128]{2,1,0:T(2,128)S(1)} %get-tuple-element.185, ...), kind=kOutput, calls=%fused_computation.236 | convolution fusion | flops 36700160 | bytes 229376 | tf_op jit(solution)/shard_map/ztpc,kztc->kztp/dot_general | solution.py:175
  98.6 5.7 %multiply_reduce_fusion.18 = (f32[16,2,128]{2,1,0:T(2,128)S(1)}, f32[16,2,128]{2,1,0:T(2,128)S(1)}) fusion(f32[16,2,128]{2,1,0:T(2,128)S(1)} %get-tuple-element.113, f32[16,2,128]{2,1,0:T(2,128)S(1)} %get-tuple-element.176, f32[16,2]{1,0:T(8,128)S(1)} %copy.88, f32[16,2,128]{2,1,0:T(2,128)S(1)} %get-tuple-element.109, f32[16,2,128]{2,1,0:T(2,128)S(1)} %fusion.134, ...), kind=kLoop, calls=%fused_computation.209 | loop fusion | flops 14671872 | bytes 229504 | tf_op jit(solution)/shard_map/reduce_sum | solution.py:92
  104.2 5.7 %multiply_reduce_fusion.20 = (f32[16,2,128]{2,1,0:T(2,128)S(1)}, f32[16,2,128]{2,1,0:T(2,128)S(1)}) fusion(f32[16,2,128]{2,1,0:T(2,128)S(1)} %get-tuple-element.95, f32[16,2,128]{2,1,0:T(2,128)S(1)} %get-tuple-element.176, f32[16,2]{1,0:T(8,128)S(1)} %copy.86, f32[16,2,128]{2,1,0:T(2,128)S(1)} %get-tuple-element.91, f32[16,2,128]{2,1,0:T(2,128)S(1)} %fusion.134, ...), kind=kLoop, calls=%fused_computation.216 | loop fusion | flops 14671872 | bytes 229504 | tf_op jit(solution)/shard_map/reduce_sum | solution.py:92
  109.9 5.6 %fusion.48 = (f32[16,2,128]{2,1,0:T(2,128)S(1)}, f32[16,2,128]{2,1,0:T(2,128)S(1)}) fusion(f32[16,2,128]{2,1,0:T(2,128)S(1)} %get-tuple-element.119, f32[16,2,128]{2,1,0:T(2,128)S(1)} %get-tuple-element.176, f32[16,2]{1,0:T(8,128)S(1)} %copy.85, f32[16,2,128]{2,1,0:T(2,128)S(1)} %get-tuple-element.115, f32[16,2,128]{2,1,0:T(2,128)S(1)} %fusion.134, ...), kind=kLoop, calls=%fused_computation.93 | loop fusion | flops 14147584 | bytes 229504 | tf_op jit(solution)/shard_map/reduce_sum | solution.py:92
  115.6 5.6 %fusion.29 = (f32[16,2,128]{2,1,0:T(2,128)S(1)}, f32[16,2,128]{2,1,0:T(2,128)S(1)}) fusion(f32[16,2,128]{2,1,0:T(2,128)S(1)} %get-tuple-element.101, f32[16,2,128]{2,1,0:T(2,128)S(1)} %get-tuple-element.176, f32[16,2]{1,0:T(8,128)S(1)} %copy.83, f32[16,2,128]{2,1,0:T(2,128)S(1)} %get-tuple-element.97, f32[16,2,128]{2,1,0:T(2,128)S(1)} %fusion.134, ...), kind=kLoop, calls=%fused_computation.74 | loop fusion | flops 14147584 | bytes 229504 | tf_op jit(solution)/shard_map/reduce_sum | solution.py:92
  121.2 5.7 %multiply_reduce_fusion.21 = (f32[16,2,128]{2,1,0:T(2,128)S(1)}, f32[16,2,128]{2,1,0:T(2,128)S(1)}) fusion(f32[16,2,128]{2,1,0:T(2,128)S(1)} %get-tuple-element.125, f32[16,2,128]{2,1,0:T(2,128)S(1)} %get-tuple-element.176, f32[16,2]{1,0:T(8,128)S(1)} %copy.82, f32[16,2,128]{2,1,0:T(2,128)S(1)} %get-tuple-element.121, f32[16,2,128]{2,1,0:T(2,128)S(1)} %fusion.134, ...), kind=kLoop, calls=%fused_computation.224 | loop fusion | flops 14671872 | bytes 229504 | tf_op jit(solution)/shard_map/reduce_sum | solution.py:92
  126.9 5.7 %multiply_reduce_fusion.23 = (f32[16,2,128]{2,1,0:T(2,128)S(1)}, f32[16,2,128]{2,1,0:T(2,128)S(1)}) fusion(f32[16,2,128]{2,1,0:T(2,128)S(1)} %get-tuple-element.107, f32[16,2,128]{2,1,0:T(2,128)S(1)} %get-tuple-element.176, f32[16,2]{1,0:T(8,128)S(1)} %copy.80, f32[16,2,128]{2,1,0:T(2,128)S(1)} %get-tuple-element.103, f32[16,2,128]{2,1,0:T(2,128)S(1)} %fusion.134, ...), kind=kLoop, calls=%fused_computation.231 | loop fusion | flops 14671872 | bytes 229504 | tf_op jit(solution)/shard_map/reduce_sum | solution.py:92
  133.1 1.3 collective-permute-start.5
  134.7 8.7 %fusion.126 = f32[2,16,2,256]{3,0,2,1:T(2,128)S(1)} fusion(f32[16,2,128]{2,1,0:T(2,128)S(1)} %get-tuple-element.182, s32[16,2,128]{2,1,0:T(2,128)S(1)} %get-tuple-element.184, f32[16,2,128]{2,1,0:T(2,128)S(1)} %get-tuple-element.181, s32[16,2,128]{2,1,0:T(2,128)S(1)} %get-tuple-element.185, f32[16,2,128]{2,1,0:T(2,128)S(1)} %get-tuple-element.180, ...), kind=kOutput, calls=%fused_computation.235 | convolution fusion | flops 36700160 | bytes 229376 | tf_op jit(solution)/shard_map/ztpc,kztp->kztc/dot_general | solution.py:200
  144.1 6.0 %psum.28 = f32[2]{0:T(128)S(1)} all-reduce(f32[2]{0:T(128)S(1)} %get-tuple-element.42), channel_id=1, replica_groups=mesh['across'=4,'along'=8,'gas_0'=4,'gas_1'=2] {'across'}, use_global_device_ids=true, to_apply=%region_42.43 | all-reduce | flops 2 | bytes 16 | tf_op jit(solution)/shard_map/psum | solution.py:65
  150.3 13.1 %psum.29 = f32[2]{0:T(128)S(1)} all-reduce(f32[2]{0:T(128)S(1)} %psum.28), channel_id=1, replica_groups=mesh['across'=4,'along'=8,'gas_0'=4,'gas_1'=2] {'along'}, use_global_device_ids=true, to_apply=%region_43.44 | all-reduce | flops 2 | bytes 16 | tf_op jit(solution)/shard_map/psum | solution.py:65
  163.4 0.9 reshape.471
  164.3 7.2 %psum.30 = f32[2]{0:T(128)S(1)} all-reduce(f32[2]{0:T(128)S(1)} %psum.29), channel_id=1, replica_groups=mesh['across'=4,'along'=8,'gas_0'=4,'gas_1'=2] {'gas_0'}, use_global_device_ids=true, to_apply=%region_44.45 | all-reduce | flops 2 | bytes 16 | tf_op jit(solution)/shard_map/psum | solution.py:65
  171.5 11.9 %all-to-all-start.1 = ((f32[8,1,2048]{2,1,0:T(1,128)}), f32[8,1,2048]{2,1,0:T(1,128)S(1)}, u32[]{:S(2)}, u32[]{:S(2)}) async-start(f32[8,1,2048]{2,1,0:T(1,128)} %reshape.471), calls=%async_computation.1 | async-start | bytes 131072 | tf_op jit(solution)/shard_map/all_to_all | solution.py:205
  183.4 2.5 psum.31
  185.9 1.9 collective-permute-start.9
  188.0 2.1 collective-permute-start.6
  190.1 8.2 %multiply_reduce_fusion.10 = (f32[16,2,128]{2,1,0:T(2,128)S(1)}, f32[16,2,128]{2,1,0:T(2,128)S(1)}, f32[16,2,128]{2,1,0:T(2,128)S(1)}, f32[16,2,128]{2,1,0:T(2,128)S(1)}) fusion(f32[16,2,128]{2,1,0:T(2,128)S(1)} %get-tuple-element.139, f32[16,2,128]{2,1,0:T(2,128)S(1)} %get-tuple-element.171, f32[16,2]{1,0:T(8,128)S(1)} %copy.81, ...), kind=kLoop, calls=%fused_computation.178 | loop fusion | flops 27770880 | bytes 262400 | tf_op jit(solution)/shard_map/reduce_sum | solution.py:92
  198.4 5.7 %multiply_reduce_fusion.7 = (f32[16,2,128]{2,1,0:T(2,128)S(1)}, f32[16,2,128]{2,1,0:T(2,128)S(1)}) fusion(f32[16,2,128]{2,1,0:T(2,128)S(1)} %get-tuple-element.144, f32[16,2,128]{2,1,0:T(2,128)S(1)} %get-tuple-element.171, f32[16,2]{1,0:T(8,128)S(1)} %copy.87, f32[16,2,128]{2,1,0:T(2,128)S(1)} %get-tuple-element.145, f32[16,2,128]{2,1,0:T(2,128)S(1)} %fusion.134, ...), kind=kLoop, calls=%fused_computation.163 | loop fusion | flops 14147584 | bytes 229504 | tf_op jit(solution)/shard_map/reduce_sum | solution.py:92
  204.1 0.8 reduce.1
  205.4 2.3 collective-permute-start.7
  207.8 0.8 multiply_add_fusion
  208.5 2.4 collective-permute-done.7
  211.3 5.7 %multiply_reduce_fusion.6 = (f32[16,2,128]{2,1,0:T(2,128)S(1)}, f32[16,2,128]{2,1,0:T(2,128)S(1)}) fusion(f32[16,2,128]{2,1,0:T(2,128)S(1)} %get-tuple-element.77, f32[16,2,128]{2,1,0:T(2,128)S(1)} %get-tuple-element.171, f32[16,2]{1,0:T(8,128)S(1)} %copy.88, f32[16,2,128]{2,1,0:T(2,128)S(1)} %get-tuple-element.73, f32[16,2,128]{2,1,0:T(2,128)S(1)} %fusion.134, ...), kind=kLoop, calls=%fused_computation.159 | loop fusion | flops 14671872 | bytes 229504 | tf_op jit(solution)/shard_map/reduce_sum | solution.py:92
  217.0 5.7 %multiply_reduce_fusion.8 = (f32[16,2,128]{2,1,0:T(2,128)S(1)}, f32[16,2,128]{2,1,0:T(2,128)S(1)}) fusion(f32[16,2,128]{2,1,0:T(2,128)S(1)} %get-tuple-element.59, f32[16,2,128]{2,1,0:T(2,128)S(1)} %get-tuple-element.171, f32[16,2]{1,0:T(8,128)S(1)} %copy.86, f32[16,2,128]{2,1,0:T(2,128)S(1)} %get-tuple-element.55, f32[16,2,128]{2,1,0:T(2,128)S(1)} %fusion.134, ...), kind=kLoop, calls=%fused_computation.166 | loop fusion | flops 14671872 | bytes 229504 | tf_op jit(solution)/shard_map/reduce_sum | solution.py:92
  222.6 5.6 %fusion.97 = (f32[16,2,128]{2,1,0:T(2,128)S(1)}, f32[16,2,128]{2,1,0:T(2,128)S(1)}) fusion(f32[16,2,128]{2,1,0:T(2,128)S(1)} %get-tuple-element.83, f32[16,2,128]{2,1,0:T(2,128)S(1)} %get-tuple-element.171, f32[16,2]{1,0:T(8,128)S(1)} %copy.85, f32[16,2,128]{2,1,0:T(2,128)S(1)} %get-tuple-element.79, f32[16,2,128]{2,1,0:T(2,128)S(1)} %fusion.134, ...), kind=kLoop, calls=%fused_computation.142 | loop fusion | flops 14147584 | bytes 229504 | tf_op jit(solution)/shard_map/reduce_sum | solution.py:92
  228.3 5.6 %fusion.78 = (f32[16,2,128]{2,1,0:T(2,128)S(1)}, f32[16,2,128]{2,1,0:T(2,128)S(1)}) fusion(f32[16,2,128]{2,1,0:T(2,128)S(1)} %get-tuple-element.65, f32[16,2,128]{2,1,0:T(2,128)S(1)} %get-tuple-element.171, f32[16,2]{1,0:T(8,128)S(1)} %copy.83, f32[16,2,128]{2,1,0:T(2,128)S(1)} %get-tuple-element.61, f32[16,2,128]{2,1,0:T(2,128)S(1)} %fusion.134, ...), kind=kLoop, calls=%fused_computation.123 | loop fusion | flops 14147584 | bytes 229504 | tf_op jit(solution)/shard_map/reduce_sum | solution.py:92
  233.9 5.7 %multiply_reduce_fusion.9 = (f32[16,2,128]{2,1,0:T(2,128)S(1)}, f32[16,2,128]{2,1,0:T(2,128)S(1)}) fusion(f32[16,2,128]{2,1,0:T(2,128)S(1)} %get-tuple-element.89, f32[16,2,128]{2,1,0:T(2,128)S(1)} %get-tuple-element.171, f32[16,2]{1,0:T(8,128)S(1)} %copy.82, f32[16,2,128]{2,1,0:T(2,128)S(1)} %get-tuple-element.85, f32[16,2,128]{2,1,0:T(2,128)S(1)} %fusion.134, ...), kind=kLoop, calls=%fused_computation.174 | loop fusion | flops 14671872 | bytes 229504 | tf_op jit(solution)/shard_map/reduce_sum | solution.py:92
  239.6 5.7 %multiply_reduce_fusion.11 = (f32[16,2,128]{2,1,0:T(2,128)S(1)}, f32[16,2,128]{2,1,0:T(2,128)S(1)}) fusion(f32[16,2,128]{2,1,0:T(2,128)S(1)} %get-tuple-element.71, f32[16,2,128]{2,1,0:T(2,128)S(1)} %get-tuple-element.171, f32[16,2]{1,0:T(8,128)S(1)} %copy.80, f32[16,2,128]{2,1,0:T(2,128)S(1)} %get-tuple-element.67, f32[16,2,128]{2,1,0:T(2,128)S(1)} %fusion.134, ...), kind=kLoop, calls=%fused_computation.181 | loop fusion | flops 14671872 | bytes 229504 | tf_op jit(solution)/shard_map/reduce_sum | solution.py:92
  245.5 0.7 pad_maximum_fusion.8
  (101 shorter events, 6.1 us)
Async XLA Ops:
  0.6 14.1 %copy-start = (f32[2,32,256]{2,1,0:T(8,128)S(1)}, f32[2,32,256]{2,1,0:T(8,128)}, u32[]{:S(2)}) copy-start(f32[2,32,256]{2,1,0:T(8,128)} %param.10) | copy-start | bytes 196612
  0.6 8.6 %copy-start.9 = (s32[16,2]{0,1:T(2,128)S(1)}, s32[16,2]{0,1:T(2,128)}, u32[]{:S(2)}) copy-start(s32[16,2]{0,1:T(2,128)} %param.16) | copy-start | bytes 388
  0.7 8.7 %copy-start.3 = (f32[2,16,2,128]{3,2,1,0:T(2,128)S(1)}, f32[2,16,2,128]{3,2,1,0:T(2,128)}, u32[]{:S(2)}) copy-start(f32[2,16,2,128]{3,2,1,0:T(2,128)} %param.12) | copy-start | bytes 98308
  0.7 8.7 %copy-start.1 = (f32[2,16,2,128]{3,2,1,0:T(2,128)S(1)}, f32[2,16,2,128]{3,2,1,0:T(2,128)}, u32[]{:S(2)}) copy-start(f32[2,16,2,128]{3,2,1,0:T(2,128)} %param.13) | copy-start | bytes 98308
  0.7 8.7 %copy-start.2 = (f32[16,2,128]{2,1,0:T(2,128)S(1)}, f32[16,2,128]{2,1,0:T(2,128)}, u32[]{:S(2)}) copy-start(f32[16,2,128]{2,1,0:T(2,128)} %param.14) | copy-start | bytes 49156
  1.7 18.1 %copy-start.6 = (s32[2,16,2,128]{3,2,1,0:T(2,128)S(1)}, s32[2,16,2,128]{3,2,1,0:T(2,128)}, u32[]{:S(2)}) copy-start(s32[2,16,2,128]{3,2,1,0:T(2,128)} %param.19) | copy-start | bytes 98308
  1.7 18.2 %copy-start.5 = (f32[32,256]{1,0:T(8,128)S(1)}, f32[32,256]{1,0:T(8,128)}, u32[]{:S(2)}) copy-start(f32[32,256]{1,0:T(8,128)} %param.11) | copy-start | bytes 98308
  1.8 18.8 %copy-start.7 = (s32[16,2,128]{2,1,0:T(2,128)S(1)}, s32[16,2,128]{2,1,0:T(2,128)}, u32[]{:S(2)}) copy-start(s32[16,2,128]{2,1,0:T(2,128)} %param.18) | copy-start | bytes 49156
  2.7 52.1 %copy-start.8 = (s32[16,2,9]{0,1,2:T(2,128)S(1)}, s32[16,2,9]{0,1,2:T(2,128)}, u32[]{:S(2)}) copy-start(s32[16,2,9]{0,1,2:T(2,128)} %param.17) | copy-start | bytes 3460
  2.7 82.8 %all-to-all-start = ((f32[8,1,2048]{2,1,0:T(1,128)}), f32[8,1,2048]{2,1,0:T(1,128)S(1)}, u32[]{:S(2)}, u32[]{:S(2)}) async-start(f32[8,1,2048]{2,1,0:T(1,128)} %reshape.469), calls=%async_computation | async-start | bytes 131072 | tf_op jit(solution)/shard_map/all_to_all | solution.py:169
  9.5 57.2 %collective-permute-start.1 = (f32[6,1,2,128]{3,2,1,0:T(2,128)S(1)}, f32[6,1,2,128]{3,2,1,0:T(2,128)S(1)}, u32[]{:S(2)}, u32[]{:S(2)}) collective-permute-start(f32[6,1,2,128]{3,2,1,0:T(2,128)S(1)} %get-tuple-element.161), channel_id=1, source_target_pairs={{8,0},{16,8},{24,16},{32,24},{40,32},{48,40},{56,48},{0,56},{9,1},... | collective-permute-start | bytes 18440 | tf_op jit(solution)/shard_map/ppermute | solution.py:38
  14.7 52.1 %collective-permute-start = (f32[6,1,2,128]{3,2,1,0:T(2,128)S(1)}, f32[6,1,2,128]{3,2,1,0:T(2,128)S(1)}, u32[]{:S(2)}, u32[]{:S(2)}) collective-permute-start(f32[6,1,2,128]{3,2,1,0:T(2,128)S(1)} %get-tuple-element.160), channel_id=1, source_target_pairs={{0,8},{8,16},{16,24},{24,32},{32,40},{40,48},{48,56},{56,0},{1,9},... | collective-permute-start | bytes 18440 | tf_op jit(solution)/shard_map/ppermute | solution.py:37
  14.8 190.6 %collective-permute-start.11 = (f32[2,32,1]{2,1,0:T(8,128)S(1)}, f32[2,32,1]{2,1,0:T(8,128)S(1)}, u32[]{:S(2)}, u32[]{:S(2)}) collective-permute-start(f32[2,32,1]{2,1,0:T(8,128)S(1)} %get-tuple-element.169), channel_id=1, source_target_pairs={{0,64},{64,128},{128,192},{1,65},{65,129},{129,193},{2,66},{66,130... | collective-permute-start | bytes 776 | tf_op jit(solution)/shard_map/ppermute | solution.py:37
  17.9 189.8 %collective-permute-start.10 = (f32[2,32,1]{2,1,0:T(8,128)S(1)}, f32[2,32,1]{2,1,0:T(8,128)S(1)}, u32[]{:S(2)}, u32[]{:S(2)}) collective-permute-start(f32[2,32,1]{2,1,0:T(8,128)S(1)} %get-tuple-element.168), channel_id=1, source_target_pairs={{64,0},{128,64},{192,128},{65,1},{129,65},{193,129},{66,2},{130,66... | collective-permute-start | bytes 776 | tf_op jit(solution)/shard_map/ppermute | solution.py:38
  19.2 188.5 %collective-permute-start.8 = (f32[2,1,256]{2,1,0:T(1,128)S(1)}, f32[2,1,256]{2,1,0:T(1,128)S(1)}, u32[]{:S(2)}, u32[]{:S(2)}) collective-permute-start(f32[2,1,256]{2,1,0:T(1,128)S(1)} %get-tuple-element.167), channel_id=1, source_target_pairs={{1,0},{2,1},{3,2},{4,3},{5,4},{6,5},{7,6},{8,7},{9,8},{10,9},{11,1... | collective-permute-start | bytes 6152 | tf_op jit(solution)/shard_map/ppermute | solution.py:52
  67.0 31.2 %collective-permute-start.2 = (f32[6,18,1,128]{3,2,1,0:T(1,128)S(1)}, f32[6,18,1,128]{3,2,1,0:T(1,128)S(1)}, u32[]{:S(2)}, u32[]{:S(2)}) collective-permute-start(f32[6,18,1,128]{3,2,1,0:T(1,128)S(1)} %get-tuple-element.132), channel_id=1, source_target_pairs={{0,1},{1,2},{2,3},{3,4},{4,5},{5,6},{6,7},{7,64},{64,65},{65,66},{... | collective-permute-start | bytes 165896 | tf_op jit(solution)/shard_map/ppermute | solution.py:51
  68.9 29.3 %collective-permute-start.3 = (f32[6,18,1,128]{3,2,1,0:T(1,128)S(1)}, f32[6,18,1,128]{3,2,1,0:T(1,128)S(1)}, u32[]{:S(2)}, u32[]{:S(2)}) collective-permute-start(f32[6,18,1,128]{3,2,1,0:T(1,128)S(1)} %get-tuple-element.133), channel_id=1, source_target_pairs={{1,0},{2,1},{3,2},{4,3},{5,4},{6,5},{7,6},{64,7},{65,64},{66,65},{... | collective-permute-start | bytes 165896 | tf_op jit(solution)/shard_map/ppermute | solution.py:52
  126.9 5.7 %copy-start.4 = (f32[16,2,128]{2,1,0:T(2,128)S(1)}, f32[16,2,128]{2,1,0:T(2,128)}, u32[]{:S(2)}) copy-start(f32[16,2,128]{2,1,0:T(2,128)} %param.15) | copy-start | bytes 49156
  133.1 52.8 %collective-permute-start.5 = (f32[6,1,2,128]{3,2,1,0:T(2,128)S(1)}, f32[6,1,2,128]{3,2,1,0:T(2,128)S(1)}, u32[]{:S(2)}, u32[]{:S(2)}) collective-permute-start(f32[6,1,2,128]{3,2,1,0:T(2,128)S(1)} %get-tuple-element.159), channel_id=1, source_target_pairs={{8,0},{16,8},{24,16},{32,24},{40,32},{48,40},{56,48},{0,56},{9,1},... | collective-permute-start | bytes 18440 | tf_op jit(solution)/shard_map/ppermute | solution.py:38
  134.4 53.5 %collective-permute-start.4 = (f32[6,1,2,128]{3,2,1,0:T(2,128)S(1)}, f32[6,1,2,128]{3,2,1,0:T(2,128)S(1)}, u32[]{:S(2)}, u32[]{:S(2)}) collective-permute-start(f32[6,1,2,128]{3,2,1,0:T(2,128)S(1)} %get-tuple-element.158), channel_id=1, source_target_pairs={{0,8},{8,16},{16,24},{24,32},{32,40},{40,48},{48,56},{56,0},{1,9},... | collective-permute-start | bytes 18440 | tf_op jit(solution)/shard_map/ppermute | solution.py:37
  171.5 32.6 %all-to-all-start.1 = ((f32[8,1,2048]{2,1,0:T(1,128)}), f32[8,1,2048]{2,1,0:T(1,128)S(1)}, u32[]{:S(2)}, u32[]{:S(2)}) async-start(f32[8,1,2048]{2,1,0:T(1,128)} %reshape.471), calls=%async_computation.1 | async-start | bytes 131072 | tf_op jit(solution)/shard_map/all_to_all | solution.py:205
  185.9 21.8 %collective-permute-start.9 = (f32[2,1,256]{2,1,0:T(1,128)S(1)}, f32[2,1,256]{2,1,0:T(1,128)S(1)}, u32[]{:S(2)}, u32[]{:S(2)}) collective-permute-start(f32[2,1,256]{2,1,0:T(1,128)S(1)} %get-tuple-element.166), channel_id=1, source_target_pairs={{0,1},{1,2},{2,3},{3,4},{4,5},{5,6},{6,7},{7,8},{8,9},{9,10},{10,1... | collective-permute-start | bytes 6152 | tf_op jit(solution)/shard_map/ppermute | solution.py:51
  188.0 20.5 %collective-permute-start.6 = (f32[6,18,1,128]{3,2,1,0:T(1,128)S(1)}, f32[6,18,1,128]{3,2,1,0:T(1,128)S(1)}, u32[]{:S(2)}, u32[]{:S(2)}) collective-permute-start(f32[6,18,1,128]{3,2,1,0:T(1,128)S(1)} %get-tuple-element.128), channel_id=1, source_target_pairs={{0,1},{1,2},{2,3},{3,4},{4,5},{5,6},{6,7},{7,64},{64,65},{65,66},{... | collective-permute-start | bytes 165896 | tf_op jit(solution)/shard_map/ppermute | solution.py:51
  205.4 5.5 %collective-permute-start.7 = (f32[6,18,1,128]{3,2,1,0:T(1,128)S(1)}, f32[6,18,1,128]{3,2,1,0:T(1,128)S(1)}, u32[]{:S(2)}, u32[]{:S(2)}) collective-permute-start(f32[6,18,1,128]{3,2,1,0:T(1,128)S(1)} %get-tuple-element.129), channel_id=1, source_target_pairs={{1,0},{2,1},{3,2},{4,3},{5,4},{6,5},{7,6},{64,7},{65,64},{66,65},{... | collective-permute-start | bytes 165896 | tf_op jit(solution)/shard_map/ppermute | solution.py:52
where the time goes:
time: 248 us; the launch traced here: 246 us
  other arithmetic  101 us (41%)
  blocking collectives  73.4 us (30%)
  starting transfers between devices  41 us (17%)
  matrix products  18.8 us (8%)
  local copies, waits for them, and re-layouts  7.45 us (3%)
    reduce_sum x16, other arithmetic, contact(): forces_z = forces_z + jnp.sum(strength * apart_z, axis=-1)  95.7 us
    pmax x4, blocking collectives, by_axis(): x = lax.pmax(x, axis)  44.7 us
    psum x4, blocking collectives, over_axes(): x = lax.psum(x, axis)  28.8 us
    all_to_all x1, starting transfers between devices, body(): lax.all_to_all(block_deposit, GAS, split_axis=1, concat_axis=2, tiled=True)  11.9 us
    dot_general x1, matrix products, body(): jnp.einsum('ztpc,kztc->kztp', weights, tile_velocity, precision=lax.Preci...  10.2 us
    dot_general x1, matrix products, body(): jnp.einsum('ztpc,kztp->kztc', weights, mean_drag, precision=lax.Precision...  8.66 us
    ppermute x3, starting transfers between devices, extended_2(): after = lax.ppermute(first, axis, down)  7.75 us
    all_to_all x1, starting transfers between devices, body(): lax.all_to_all(gas_vel, GAS, split_axis=2, concat_axis=1, tiled=True)  6.59 us
  transfers between devices with their start and end apart: 14, of which 1 were waited for; matrix products, arithmetic and copies ran while one was open for 37% of the time, Pallas kernels for 0%

commit v1 on v0

v1 whole, which is shorter than its diff:
```python
import functools

import jax
import jax.numpy as jnp
from jax import lax
from jax.experimental import pallas as pl
from jax.experimental.pallas import tpu as pltpu
from jax.sharding import PartitionSpec as P

ALONG_GAS = ("along", "gas")
ACROSS_GAS = ("across", "gas")
MESH_ID = pl.DeviceIdType.MESH
OFFSETS = [(-1, -1), (-1, 0), (-1, 1), (0, -1), (0, 0), (0, 1), (1, -1), (1, 0), (1, 1)]
DEAD = -16384.0
F32 = jnp.float32
BF16 = jnp.bfloat16
VMEM_SPEC = pl.BlockSpec(memory_space=pltpu.VMEM)
SMEM_SPEC = pl.BlockSpec(memory_space=pltpu.SMEM)
N_ACROSS, N_ALONG, N_GAS = 4, 8, 8


def iota(shape, dim):
    return lax.broadcasted_iota(jnp.int32, shape, dim)


def ext_row(ii, jj):
    base = {-1: 32, 0: 0, 1: 16, 2: 48}[jj]
    return jnp.where(ii < 0, 64 + 8 * (jj + 1) + 7, jnp.where(ii > 15, 96 + 8 * (jj + 1), base + ii))


def prep_kernel(gas, visc, pos, vel, rad, counts, st, gp, mx):
    rate = jnp.abs(gas[0]) + jnp.abs(gas[1]) + 4.0 * visc[...]
    top = jnp.max(jnp.max(rate, axis=1, keepdims=True), axis=0, keepdims=True)
    mx[...] = jnp.broadcast_to(top, (8, 128))
    lane = iota((16, 128), 1)
    for g in range(N_GAS):
        blk = slice((g // 4) * 128, (g // 4) * 128 + 128)
        off = (g % 4) * 32
        for k in range(2):
            low = gas[k, 0:16, blk]
            high = gas[k, 16:32, blk]
            low = pltpu.roll(low, (128 - off) % 128, 1) if off else low
            shift = (160 - off) % 128
            high = pltpu.roll(high, shift, 1) if shift else high
            piece = jnp.where(lane < 32, low, jnp.where(lane < 64, high, 0.0))
            gp[g, k * 16:(k + 1) * 16, :] = piece
    lane32 = iota((16, 128), 1)
    row16 = iota((16, 128), 0)
    for j in range(2):
        rows = slice(j * 16, (j + 1) * 16)
        take = pl.ds(j, 16, stride=2)
        cnt = jnp.zeros((16, 128), jnp.int32)
        for i in range(16):
            cnt = jnp.where(row16 == i, counts[j, i], cnt)
        st[0, rows, :] = pos[0, take, :] * 16.0
        st[1, rows, :] = pos[1, take, :] * 16.0
        st[2, rows, :] = vel[0, take, :]
        st[3, rows, :] = vel[1, take, :]
        st[4, rows, :] = jnp.where(lane32 < cnt, rad[take, :], DEAD)
        st[5, rows, :] = cnt.astype(F32)
    st[6] = jnp.zeros((32, 128), F32)
    st[7] = jnp.zeros((32, 128), F32)


def comm_kernel(first, *refs):
    if first:
        (st, pc, mx, gas, ext, pv, red, gr, gc, mb, m1, m2,
         own_sem, hs, hr, ps, pr, rs, rr, es, er) = refs
    else:
        (st, pc, mx, ext, pv, red, mb, m1, m2,
         own_sem, hs, hr, ps, pr, rs, rr) = refs
    ax, al, g = lax.axis_index("across"), lax.axis_index("along"), lax.axis_index("gas")
    up, down = lax.rem(al + 1, N_ALONG), lax.rem(al + N_ALONG - 1, N_ALONG)
    lin = ax * N_GAS + g
    has_left, has_right = lin > 0, lin < N_ACROSS * N_GAS - 1
    left = jnp.maximum(lin - 1, 0)
    right = jnp.minimum(lin + 1, N_ACROSS * N_GAS - 1)

    def col(index, along):
        return {"across": lax.div(index, N_GAS), "along": along, "gas": lax.rem(index, N_GAS)}

    slab = al * N_GAS + g
    slabs = N_ALONG * N_GAS
    after, before = lax.rem(slab + 1, slabs), lax.rem(slab + slabs - 1, slabs)

    def slab_id(index):
        return {"across": ax, "along": lax.div(index, N_GAS), "gas": lax.rem(index, N_GAS)}

    barrier = pltpu.get_barrier_semaphore()

    def greet(device):
        pl.semaphore_signal(barrier, inc=1, device_id=device, device_id_type=MESH_ID)

    for k in range(1, N_ACROSS):
        greet({"across": lax.rem(ax + k, N_ACROSS)})
    for k in range(1, N_GAS):
        greet({"gas": lax.rem(g + k, N_GAS)})
    for k in range(1, N_ALONG):
        greet({"along": lax.rem(al + k, N_ALONG)})
    expect = N_ACROSS + N_GAS + N_ALONG - 3
    if first:
        greet(slab_id(after))
        greet(slab_id(before))
        expect += 2

    @pl.when(has_left)
    def _():
        for along in (down, al, up):
            greet(col(left, along))

    @pl.when(has_right)
    def _():
        for along in (down, al, up):
            greet(col(right, along))

    own = pltpu.make_async_copy(st, ext.at[:, pl.ds(0, 32)], own_sem.at[0])
    own.start()
    own_piece = pltpu.make_async_copy(pc.at[g], pv.at[g], own_sem.at[1])
    own_piece.start()

    @pl.when(jnp.logical_not(has_left))
    def _():
        ext[:, 32:48, :] = jnp.zeros((8, 16, 128), F32)
        ext[:, 64:72, :] = jnp.zeros((8, 8, 128), F32)
        ext[:, 96:104, :] = jnp.zeros((8, 8, 128), F32)

    @pl.when(jnp.logical_not(has_right))
    def _():
        ext[:, 48:64, :] = jnp.zeros((8, 16, 128), F32)
        ext[:, 88:96, :] = jnp.zeros((8, 8, 128), F32)
        ext[:, 120:128, :] = jnp.zeros((8, 8, 128), F32)

    if first:
        @pl.when(ax == 0)
        def _():
            gc[0] = jnp.zeros((2, 32, 128), F32)

        @pl.when(ax == N_ACROSS - 1)
        def _():
            gc[1] = jnp.zeros((2, 32, 128), F32)

    sides = jnp.where(has_left, 3, 0) + jnp.where(has_right, 3, 0)
    pl.semaphore_wait(barrier, expect + sides)

    def remote(src, dst, send, recv, device):
        return pltpu.make_async_remote_copy(
            src_ref=src, dst_ref=dst, send_sem=send, recv_sem=recv,
            device_id=device, device_id_type=MESH_ID,
        )

    def reduce_sends(phase, src, axis, me, size):
        out = []
        for k in range(1, size):
            out.append(remote(src, mb.at[phase, me], rs.at[phase, k], rr.at[phase, k],
                              {axis: lax.rem(me + k, size)}))
        for c in out:
            c.start()
        return out

    phase0 = reduce_sends(0, mx, "across", ax, N_ACROSS)

    def halo(c, src_rows, size, dst_row, device):
        return remote(st.at[pl.ds(0, 6), pl.ds(src_rows, size)],
                      ext.at[pl.ds(0, 6), pl.ds(dst_row, size)], hs.at[c], hr.at[c], device)

    lefts = [halo(0, 0, 16, 48, col(left, al)),
             halo(1, 8, 8, 64 + 24, col(left, up)),
             halo(2, 0, 8, 96 + 24, col(left, down))]
    rights = [halo(3, 16, 16, 32, col(right, al)),
              halo(4, 24, 8, 64, col(right, up)),
              halo(5, 16, 8, 96, col(right, down))]
    rows = [halo(6, 8, 8, 64 + 8, {"along": up}),
            halo(7, 24, 8, 64 + 16, {"along": up}),
            halo(8, 0, 8, 96 + 8, {"along": down}),
            halo(9, 16, 8, 96 + 16, {"along": down})]

    @pl.when(has_left)
    def _():
        for c in lefts:
            c.start()

    @pl.when(has_right)
    def _():
        for c in rights:
            c.start()

    for c in rows:
        c.start()
    pieces = []
    for k in range(1, N_GAS):
        peer = lax.rem(g + k, N_GAS)
        c = remote(pc.at[peer], pv.at[g], ps.at[k], pr.at[k], {"gas": peer})
        c.start()
        pieces.append(c)
    if first:
        edges = [remote(gas.at[:, pl.ds(24, 8)], gr.at[0], es.at[0], er.at[0], slab_id(after)),
                 remote(gas.at[:, pl.ds(0, 8)], gr.at[1], es.at[1], er.at[1], slab_id(before))]
        for c in edges:
            c.start()
        to_right = remote(gas.at[:, :, pl.ds(128, 128)], gc.at[0], es.at[2], er.at[2],
                          {"across": jnp.minimum(ax + 1, N_ACROSS - 1)})
        to_left = remote(gas.at[:, :, pl.ds(0, 128)], gc.at[1], es.at[3], er.at[3],
                         {"across": jnp.maximum(ax - 1, 0)})

        @pl.when(ax < N_ACROSS - 1)
        def _():
            to_right.start()

        @pl.when(ax > 0)
        def _():
            to_left.start()

    def combine(phase, mine, me, size, copies):
        for c in copies:
            c.wait_recv()
        mb[phase, me] = mine
        total = mb[phase, 0]
        for k in range(1, size):
            total = jnp.maximum(total, mb[phase, k]) if first else total + mb[phase, k]
        return total

    m1[...] = combine(0, mx[...], ax, N_ACROSS, phase0)
    phase1 = reduce_sends(1, m1, "gas", g, N_GAS)
    m2[...] = combine(1, m1[...], g, N_GAS, phase1)
    phase2 = reduce_sends(2, m2, "along", al, N_ALONG)
    red[...] = combine(2, m2[...], al, N_ALONG, phase2)

    own.wait()
    own_piece.wait()
    for c in phase0 + phase1 + phase2:
        c.wait_send()
    for c in rows + pieces:
        c.wait()

    @pl.when(has_left)
    def _():
        for c in lefts:
            c.wait_send()
        for c in rights:
            c.wait_recv()

    @pl.when(has_right)
    def _():
        for c in rights:
            c.wait_send()
        for c in lefts:
            c.wait_recv()

    if first:
        for c in edges:
            c.wait()

        @pl.when(ax < N_ACROSS - 1)
        def _():
            to_right.wait_send()
            to_left.wait_recv()

        @pl.when(ax > 0)
        def _():
            to_left.wait_send()
            to_right.wait_recv()


def exchange(first, st, pc, mx, gas=None):
    out_shape = [jax.ShapeDtypeStruct((8, 128, 128), F32),
                 jax.ShapeDtypeStruct((8, 32, 128), F32),
                 jax.ShapeDtypeStruct((8, 128), F32)]
    scratch = [pltpu.VMEM((3, 8, 8, 128), F32), pltpu.VMEM((8, 128), F32), pltpu.VMEM((8, 128), F32),
               pltpu.SemaphoreType.DMA((2,)),
               pltpu.SemaphoreType.DMA((10,)), pltpu.SemaphoreType.DMA((10,)),
               pltpu.SemaphoreType.DMA((8,)), pltpu.SemaphoreType.DMA((8,)),
               pltpu.SemaphoreType.DMA((3, 8)), pltpu.SemaphoreType.DMA((3, 8))]
    args = [st, pc, mx]
    if first:
        args.append(gas)
        out_shape += [jax.ShapeDtypeStruct((2, 2, 8, 256), F32), jax.ShapeDtypeStruct((2, 2, 32, 128), F32)]
        scratch += [pltpu.SemaphoreType.DMA((4,)), pltpu.SemaphoreType.DMA((4,))]
    return pl.pallas_call(
        functools.partial(comm_kernel, first),
        out_shape=out_shape,
        in_specs=[VMEM_SPEC] * len(args),
        out_specs=[VMEM_SPEC] * len(out_shape),
        scratch_shapes=scratch,
        compiler_params=pltpu.CompilerParams(collective_id=0 if first else 1, has_side_effects=True),
        name="exchange_first" if first else "exchange_second",
    )(*args)


def split3(x):
    hi = x.astype(BF16).astype(F32)
    rest = x - hi
    mid = rest.astype(BF16).astype(F32)
    return hi, mid, rest - mid


def contact_forces(ext, pat, cnt, qt, lst, rhs, frc, sem):
    to_smem = pltpu.make_async_copy(ext.at[pl.ds(5 * 128, 128)], cnt, sem)
    to_smem.start()
    eye = (iota((128, 128), 0) == iota((128, 128), 1)).astype(BF16)
    attr_row = iota((8, 128), 0)
    tail = jnp.concatenate([jnp.zeros((8, 128), F32), jnp.ones((24, 128), F32), jnp.zeros((8, 128), F32)], axis=0)

    def parts(row):
        block = ext[pl.ds(row, 8, stride=128), :]
        return split3(jnp.where(attr_row < 5, block, 0.0))

    def transposed(row):
        hi, mid, lo = parts(row)
        rows = jnp.concatenate([hi, mid, lo, tail], axis=0).astype(BF16)
        turned = lax.dot_general(eye, rows, (((1,), (1,)), ((), ())), preferred_element_type=F32)
        start = row * 128 if isinstance(row, int) else pl.multiple_of(row * 128, 128)
        qt[pl.ds(start, 128), 0:64] = turned

    def some(step, carry):
        for u in range(4):
            transposed(step * 4 + u)
        return carry

    lax.fori_loop(0, 16, some, 0)
    for c in range(4):
        transposed(64 + 8 * c + 7)
        transposed(96 + 8 * c)

    block_of = iota((32, 640), 1) >> 7
    row_of = iota((32, 640), 0)
    attr_of = row_of & 7
    own_scale = jnp.where(block_of < 2, -1.0, jnp.where(block_of < 4, 2.0, 1.0))
    const = jnp.where((attr_of == block_of) & (row_of < 24), own_scale, 0.0)
    const = jnp.where((row_of == 24) & (block_of == 0) | (row_of == 25) & (block_of == 1), -16.0, const)
    for u in range(2):
        rhs[u, 0:32, :] = const.astype(BF16)
    to_smem.wait()
    lane = iota((8, 128), 1)

    def row_step(i, carry):
        for j in range(2):
            work = lst.at[j]
            mine = j * 16 + i
            hi, mid, lo = parts(mine)
            zero8 = jnp.zeros((8, 128), F32)
            columns = []
            for a in range(5):
                keep = attr_row == a
                scale = 1.0 if a in (0, 1, 4) else -2.0
                columns.append(jnp.concatenate(
                    [jnp.where(keep, hi * scale, 0.0), jnp.where(keep, mid * scale, 0.0),
                     jnp.where(keep, lo * scale, 0.0), zero8], axis=0))
            rhs[j, 32:64, :] = jnp.concatenate(columns, axis=1).astype(BF16)
            off = i * 0
            for n, (di, dj) in enumerate(OFFSETS):
                row = ext_row(i + di, j + dj)
                mark = jnp.where(lane == 24, float(di), jnp.where(lane == 25, float(dj), 0.0))
                start = pl.multiple_of(row * 128, 128)
                for c in range(16):
                    work[pl.ds(pl.multiple_of(off + c * 8, 8), 8), :] = (
                        qt[pl.ds(start + c * 8, 8), :] + mark)
                live = cnt[row, 0].astype(jnp.int32) * pat[n, j, i]
                off = off + ((live + 7) & -8)
            for c in range(16):
                work[pl.ds(pl.multiple_of(off + c * 8, 8), 8), :] = jnp.zeros((8, 128), F32)
            right = rhs[j]

            def block(b, acc):
                fz, fx = acc
                q = work[pl.ds(pl.multiple_of(b * 128, 128), 128), 0:64].astype(BF16)
                got = jnp.dot(q, right, preferred_element_type=F32)
                rz, rx = got[:, 0:128], got[:, 128:256]
                dz, dx = got[:, 256:384], got[:, 384:512]
                d2 = rz * rz + rx * rx + 0.0001
                inv = lax.rsqrt(d2)
                depth = jnp.maximum(got[:, 512:640] - d2 * inv, 0.0)
                push = depth * inv * (40.0 + (dz * rz + dx * rx) * inv)
                fz = fz + jnp.sum((push * rz).reshape(16, 8, 128), axis=0)
                fx = fx + jnp.sum((push * rx).reshape(16, 8, 128), axis=0)
                return fz, fx

            fz, fx = lax.fori_loop(0, (off + 127) >> 7, block, (zero8, zero8))
            frc[0, pl.ds(mine, 1), :] = jnp.sum(fz, axis=0, keepdims=True)
            frc[1, pl.ds(mine, 1), :] = jnp.sum(fx, axis=0, keepdims=True)
        return carry

    lax.fori_loop(0, 16, row_step, 0)


def by_column(ref, *lead):
    return jnp.concatenate([ref[(*lead, pl.ds(0, 16, stride=2), slice(None))],
                            ref[(*lead, pl.ds(1, 16, stride=2), slice(None))]], axis=0)


def first_kernel(ext, gv, rate, idx, frac, coef, pat, st2, dp, tot, dr2, inv_out,
                 cnt, qt, lst, rhs, frc, itp, sem):
    def weights(r, t4):
        index = idx[pl.ds(r, 1), :]
        row, column = index >> 4, index & 15
        share_z = frac[0, pl.ds(r, 1), :].astype(F32) / 1024.0
        share_x = frac[1, pl.ds(r, 1), :].astype(F32) / 1024.0
        c64 = iota((64, 128), 0) - t4 * 16
        wx = jnp.where(c64 == column, 1.0 - share_x, jnp.where(c64 == column + 1, share_x, 0.0))
        r16 = iota((16, 128), 0)
        wz = jnp.where(r16 == row, 1.0 - share_z, jnp.where(r16 == row + 1, share_z, 0.0))
        return wz, wx

    def sample(h, carry):
        field = gv[h][:, 0:64]
        for t in range(2):
            for j in range(2):
                wz, wx = weights(4 * h + 2 * t + j, t * 2 + j)
                along = jnp.dot(field, wx, precision=lax.Precision.HIGHEST, preferred_element_type=F32)
                for k in range(2):
                    itp[k, pl.ds(j * 16 + 2 * h + t, 1), :] = jnp.sum(
                        wz * along[k * 16:(k + 1) * 16], axis=0, keepdims=True)
        return carry

    lax.fori_loop(0, 8, sample, 0)
    contact_forces(ext, pat, cnt, qt, lst, rhs, frc, sem)
    step = 0.2 / rate[0:1, :]
    drag = by_column(coef)
    radius = ext[4 * 128:4 * 128 + 32, :]
    alive = jnp.where(radius > 0.0, 1.0, 0.0)
    inverse = jnp.where(radius > 0.0, 0.36 / (radius * radius), 0.0)
    inv_out[...] = inverse
    means = []
    for k in range(2):
        place = ext[k * 128:k * 128 + 32, :]
        speed = ext[(2 + k) * 128:(2 + k) * 128 + 32, :]
        drag1 = drag * (itp[k] - speed)
        speed2 = speed + step * (inverse * (frc[k] + drag1) - (alive if k == 0 else 0.0))
        st2[k] = place + step * speed2
        st2[2 + k] = speed2
        drag2 = drag * (itp[k] - speed2)
        dr2[k] = drag2
        mean = 0.5 * (alive * drag1 + alive * drag2)
        itp[k] = mean
        means.append(jnp.sum(jnp.sum(mean, axis=1, keepdims=True), axis=0, keepdims=True))
    st2[4] = radius
    st2[5] = ext[5 * 128:5 * 128 + 32, :]
    st2[6] = jnp.zeros((32, 128), F32)
    st2[7] = jnp.zeros((32, 128), F32)
    tot[...] = jnp.where(iota((8, 128), 0) == 0, means[0], means[1])

    def spread(h, carry):
        total = jnp.zeros((32, 64), F32)
        for t in range(2):
            for j in range(2):
                wz, wx = weights(4 * h + 2 * t + j, t * 2 + j)
                m0 = itp[0, pl.ds(j * 16 + 2 * h + t, 1), :]
                m1 = itp[1, pl.ds(j * 16 + 2 * h + t, 1), :]
                lhs = jnp.concatenate([wz * m0, wz * m1], axis=0)
                total = total + lax.dot_general(lhs, wx, (((1,), (1,)), ((), ())),
                                                precision=lax.Precision.HIGHEST, preferred_element_type=F32)
        dp[h, :, 0:64] = total
        dp[h, :, 64:128] = jnp.zeros((32, 64), F32)
        return carry

    lax.fori_loop(0, 8, spread, 0)


def second_kernel(ext, dv, tot, rate, dr2, inverse, gas, visc, gr, gc, pat, part, out,
                  cnt, qt, lst, rhs, frc, sem):
    contact_forces(ext, pat, cnt, qt, lst, rhs, frc, sem)
    step = 0.2 / rate[0:1, :]
    radius = ext[4 * 128:4 * 128 + 32, :]
    alive = jnp.where(radius > 0.0, 1.0, 0.0)
    for k in range(2):
        place = ext[k * 128:k * 128 + 32, :]
        speed = ext[(2 + k) * 128:(2 + k) * 128 + 32, :]
        speed2 = speed + step * (inverse[...] * (frc[k] + dr2[k]) - (alive if k == 0 else 0.0))
        place2 = (place + step * speed2) * 0.0625
        for j in range(2):
            part[k, pl.ds(j, 16, stride=2), :] = place2[j * 16:(j + 1) * 16]
            part[2 + k, pl.ds(j, 16, stride=2), :] = speed2[j * 16:(j + 1) * 16]
    gas_step = 0.4 / rate[0:1, 0:1]
    lane = iota((32, 256), 1)
    row = iota((32, 256), 0)
    lane16 = iota((16, 128), 1) >> 5
    for k in range(2):
        u = gas[k]
        upper = jnp.where(row == 31, gr[1, k, 0:1, :], pltpu.roll(u, 31, 0))
        lower = jnp.where(row == 0, gr[0, k, 7:8, :], pltpu.roll(u, 1, 0))
        right = jnp.where(lane == 255, gc[1, k, :, 0:1], pltpu.roll(u, 255, 1))
        left = jnp.where(lane == 0, gc[0, k, :, 127:128], pltpu.roll(u, 1, 1))
        laplace = upper + lower + right + left - 4.0 * u
        advect = gas[0] * (upper - lower) * 0.5 + gas[1] * (right - left) * 0.5
        quads = []
        for t in range(2):
            halves = []
            for b in range(2):
                whole = None
                for q in range(4):
                    piece = dv[4 * b + q, k * 16:(k + 1) * 16, :]
                    shift = (q * 32 - t * 32) % 128
                    piece = pltpu.roll(piece, shift, 1) if shift else piece
                    whole = piece if whole is None else jnp.where(lane16 == q, piece, whole)
                halves.append(whole)
            quads.append(jnp.concatenate(halves, axis=1))
        deposit = jnp.concatenate(quads, axis=0)
        source = tot[k:k + 1, 0:1] / 2097152.0 - deposit
        out[k] = u + gas_step * (visc[...] * laplace - advect + source)


CONTACT_SCRATCH = [
    pltpu.SMEM((128, 128), F32),
    pltpu.VMEM((128 * 128, 128), F32),
    pltpu.VMEM((2, 1408, 128), F32),
    pltpu.VMEM((2, 64, 640), BF16),
    pltpu.VMEM((2, 32, 128), F32),
]


def body(gas, visc, pos, vel, rad, coef, counts, pattern, idx, frac):
    counts_t = counts.T
    pattern_t = pattern.transpose(2, 1, 0)
    pos, vel, frac = (x.reshape(2, 32, 128) for x in (pos, vel, frac))
    rad, coef, idx = (x.reshape(32, 128) for x in (rad, coef, idx))

    def shapes(*dims):
        return [jax.ShapeDtypeStruct(d, F32) for d in dims]

    st, gp, mx = pl.pallas_call(
        prep_kernel,
        out_shape=shapes((8, 32, 128), (8, 32, 128), (8, 128)),
        in_specs=[VMEM_SPEC] * 5 + [SMEM_SPEC],
        out_specs=[VMEM_SPEC] * 3,
        name="prepare",
    )(gas, visc, pos, vel, rad, counts_t)
    ext, gv, rate, gr, gc = exchange(True, st, gp, mx, gas)
    st2, dp, tot, dr2, inverse = pl.pallas_call(
        first_kernel,
        out_shape=shapes((8, 32, 128), (8, 32, 128), (8, 128), (2, 32, 128), (32, 128)),
        in_specs=[VMEM_SPEC] * 6 + [SMEM_SPEC],
        out_specs=[VMEM_SPEC] * 5,
        scratch_shapes=CONTACT_SCRATCH + [pltpu.VMEM((2, 32, 128), F32), pltpu.SemaphoreType.DMA],
        name="first_substep",
    )(ext.reshape(1024, 128), gv, rate, idx, frac, coef, pattern_t)
    ext2, dv, total = exchange(False, st2, dp, tot)
    part, out = pl.pallas_call(
        second_kernel,
        out_shape=shapes((4, 32, 128), (2, 32, 256)),
        in_specs=[VMEM_SPEC] * 10 + [SMEM_SPEC],
        out_specs=[VMEM_SPEC] * 2,
        scratch_shapes=CONTACT_SCRATCH + [pltpu.SemaphoreType.DMA],
        name="second_substep",
    )(ext2.reshape(1024, 128), dv, total, rate, dr2, inverse, gas, visc, gr, gc, pattern_t)
    return part.reshape(4, 16, 2, 128), out


def solution(mesh):
    return jax.shard_map(
        body,
        mesh=mesh,
        in_specs=(
            P(None, ALONG_GAS, "across"),
            P(ALONG_GAS, "across"),
            P(None, "along", ACROSS_GAS, None),
            P(None, "along", ACROSS_GAS, None),
            P("along", ACROSS_GAS, None),
            P("along", ACROSS_GAS, None),
            P("along", ACROSS_GAS),
            P("along", ACROSS_GAS, None),
            P("along", ACROSS_GAS, None),
            P(None, "along", ACROSS_GAS, None),
        ),
        out_specs=(P(None, "along", ACROSS_GAS, None), P(None, ALONG_GAS, "across")),
        check_vma=False,
    )
```

time: 248 us -> 121 us (0.49)
  Pallas kernels: 0 us -> 118 us
  other arithmetic: 101 us -> 0 us
  blocking collectives: 73.4 us -> 0 us
  starting transfers between devices: 41 us -> 0 us
  matrix products: 18.8 us -> 0 us
  local copies, waits for them, and re-layouts: 7.45 us -> 0 us
    pallas_call x0 -> x5, Pallas kernels: none -> 118 us  [the longest x2 43.9 us: exchange(): pl.pallas_call(functools.partial(comm_kernel, first), out_shape=out_shape...]
    reduce_sum x17 -> x0, other arithmetic: 95.8 us -> none  [the longest x16 95.7 us: contact(): forces_z = forces_z + jnp.sum(strength * apart_z, axis=-1)]
    pmax x4 -> x0, blocking collectives: 44.7 us -> none  [by_axis(): x = lax.pmax(x, axis)]
    psum x4 -> x0, blocking collectives: 28.8 us -> none  [over_axes(): x = lax.psum(x, axis)]
    ppermute x12 -> x0, starting transfers between devices: 22.5 us -> none  [the longest x3 7.75 us: extended_2(): after = lax.ppermute(first, axis, down)]
    dot_general x2 -> x0, matrix products: 18.8 us -> none  [the longest x1 10.2 us: body(): jnp.einsum('ztpc,kztc->kztp', weights, tile_velocity, precision=lax.Preci...]
    all_to_all x2 -> x0, starting transfers between devices: 18.5 us -> none  [the longest x1 11.9 us: body(): lax.all_to_all(block_deposit, GAS, split_axis=1, concat_axis=2, tiled=True)]
    unnamed x30 -> x0, local copies, waits for them, and re-layouts: 3.5 us -> none
  transfers between devices with their start and end apart: 14 -> 0, of which waited for: 1 -> 0; matrix products, arithmetic and copies ran while one was open for 37% -> 0% of each run, Pallas kernels for 0% -> 0%
where the time goes in v1:
time: 121 us; the launch traced here: 119 us
  Pallas kernels  118 us (98%)
    pallas_call x2, Pallas kernels, exchange(): pl.pallas_call(functools.partial(comm_kernel, first), out_shape=out_shape...  43.9 us
    pallas_call x1, Pallas kernels, body(): pl.pallas_call(first_kernel, out_shape=shapes((8, 32, 128), (8, 32, 128),...  38.8 us
    pallas_call x1, Pallas kernels, body(): pl.pallas_call(second_kernel, out_shape=shapes((4, 32, 128), (2, 32, 256)...  34.1 us

profile of v1, /device:TPU:1, one launch (start us, length us, event | category | flops | bytes accessed | tf_op | source)
XLA Modules:
  0.0 119.1 jit_solution(11577020061302213237)
XLA Ops:
  0.6 1.7 %prepare.1 = (f32[8,32,128]{2,1,0:T(8,128)}, f32[8,32,128]{2,1,0:T(8,128)}, f32[8,128]{1,0:T(8,128)}) custom-call(f32[2,32,256]{2,1,0:T(8,128)} %gas.3, f32[32,256]{1,0:T(8,128)} %visc.3, f32[2,32,128]{2,1,0:T(8,128)} %bitcast.16, f32[2,32,128]{2,1,0:T(8,128)} %bitcast.17, f32[32,128]{1,0:T(8,128)} %bitcast.20, s32[2,16]{1,0:T(2,128)} %bitcast.21), custom_call_target="tpu_custom_call" | custom-call | tf_op jit(solution)/shard_map/prepare/pallas_call | solution.py:519
  2.3 23.7 %exchange_first.1 = (f32[8,128,128]{2,1,0:T(8,128)}, f32[8,32,128]{2,1,0:T(8,128)}, f32[8,128]{1,0:T(8,128)}, f32[2,2,8,256]{3,2,1,0:T(8,128)}, f32[2,2,32,128]{3,2,1,0:T(8,128)}) custom-call(f32[8,32,128]{2,1,0:T(8,128)} %get-tuple-element.20.refs_0_, f32[8,32,128]{2,1,0:T(8,128)} %get-tuple-element.21.refs_1_, f32[8,128]{1,0:T(8,128)} %get-tuple-element.22.refs_2_, ...), custom_call_target="tpu_custom_call" | custom-call | tf_op jit(solution)/shard_map/exchange_first/pallas_call | solution.py:278
  26.0 38.8 %first_substep.1 = (f32[8,32,128]{2,1,0:T(8,128)}, f32[8,32,128]{2,1,0:T(8,128)}, f32[8,128]{1,0:T(8,128)}, f32[2,32,128]{2,1,0:T(8,128)}, f32[32,128]{1,0:T(8,128)}) custom-call(f32[1024,128]{1,0:T(8,128)} %bitcast.11, f32[8,32,128]{2,1,0:T(8,128)} %get-tuple-element.24.gv, f32[8,128]{1,0:T(8,128)} %get-tuple-element.25.rate, s32[32,128]{1,0:T(8,128)} %bitcast.18, ...), custom_call_target="tpu_custom_call" | custom-call | tf_op jit(solution)/shard_map/first_substep/pallas_call | solution.py:527
  64.8 20.2 %exchange_second.1 = (f32[8,128,128]{2,1,0:T(8,128)}, f32[8,32,128]{2,1,0:T(8,128)}, f32[8,128]{1,0:T(8,128)}) custom-call(f32[8,32,128]{2,1,0:T(8,128)} %get-tuple-element.26.refs_0_, f32[8,32,128]{2,1,0:T(8,128)} %get-tuple-element.27.refs_1_, f32[8,128]{1,0:T(8,128)} %get-tuple-element.28.refs_2_), custom_call_target="tpu_custom_call" | custom-call | tf_op jit(solution)/shard_map/exchange_second/pallas_call | solution.py:278
  85.0 34.1 %second_substep.1 = (f32[4,32,128]{2,1,0:T(8,128)}, f32[2,32,256]{2,1,0:T(8,128)}) custom-call(f32[1024,128]{1,0:T(8,128)} %bitcast.12, f32[8,32,128]{2,1,0:T(8,128)} %get-tuple-element.30.dv, f32[8,128]{1,0:T(8,128)} %get-tuple-element.31.tot, f32[8,128]{1,0:T(8,128)} %get-tuple-element.25.rate, f32[2,32,128]{2,1,0:T(8,128)} %get-tuple-element.32.dr2, ...), custom_call_target="tpu_custom_call" | custom-call | tf_op jit(solution)/shard_map/second_substep/pallas_call | solution.py:536
